TPU v7x, 256 devices: a whole 4x4x8 slice. The times are simulated.
256 devices in a mesh: dp: 16 (over z_hi, x, core), fsdp: 16 (over y, z_lo).
Axes of the slice: x: 4, y: 4, z: 8 (z_hi: 2, z_lo: 4; z = z_hi * 4 + z_lo), core: 2. Of those that a mesh axis runs over, the one named last changes fastest.
Arguments:
- token_ids: int32 [32768], P('dp'), may hold values from 0 to 30527, as said below
- embed_table: bfloat16 [30528, 768], P('fsdp'), may hold values from -16 to 16, as said below
- w_qkv: bfloat16 [768, 2304], P('fsdp'), may hold values from -2 to 2
- w_out: bfloat16 [768, 768], P('fsdp'), may hold values from -0.21875 to 0.21875
- ln_gain: float32 [768], replicated, may hold values from 0.5 to 1.5
- ln_bias: float32 [768], replicated, may hold values from -1 to 1
- centroids_t: bfloat16 [768, 32768], P('fsdp', 'dp'), may hold values from -24 to 24
- assignments: int32 [32768], replicated, may hold values from 0 to 32767, as said below
Outputs:
- token_loss: float32 [32768], P(('dp', 'fsdp'))
- new_centroids: float32 [32768, 768], P(('dp', 'fsdp'))
Inputs may be any that keep to these rules, and one draw needn't show every extreme that they name: `token_ids`: id 0 is padding; a passage may end in a run of padding. `embed_table`: token embeddings of order one. `assignments`: cluster sizes are skewed.
All inputs are finite; a program needn't handle non-finite values.
Results may differ from a plain program's by a relative error of at most 0.0055.
Values may be sent and summed in bfloat16 or wider, within the bound.
No kernel may reach another device: no remote copies, remote signals or barrier semaphores. Data moves between devices by JAX's collectives and lax.ppermute only.
A program may use at most 64 MiB of HBM per device.

v0:
```python
import math
import jax
import jax.numpy as jnp
from jax import lax
from jax.sharding import Mesh
from jax.sharding import PartitionSpec as P

HEADS = 12
HEAD = 64
SEQ = 128
FSDP = ("fsdp_0", "fsdp_1")
DP_FSDP = ("dp", "fsdp_0", "fsdp_1")


def in_blocks(shard, dim, devices):
    before, after = (shard.shape[:dim], shard.shape[dim + 1 :])
    return jnp.moveaxis(shard.reshape(*before, devices, -1, *after), dim, 0)


def sent_and_summed(shard, axis, dim):
    devices = lax.axis_size(axis)
    parts = lax.all_to_all(in_blocks(shard, dim, devices), axis, 0, 0, tiled=True)
    return jnp.sum(parts.astype(jnp.float32), axis=0)


def in_one_piece(arrays, axis, dim, along):
    both = jnp.concatenate(arrays, axis=along)
    filled, at, done = (lax.all_gather(both, axis, axis=dim, tiled=True), 0, [])
    for a in arrays:
        done.append(lax.slice_in_dim(filled, at, at + a.shape[along], axis=along))
        at += a.shape[along]
    return tuple(done)


def sent_together(arrays, axis, split_dim, concat_dim, along):
    widths = [a.shape[along] for a in arrays]
    both = jnp.concatenate(arrays, axis=along)
    filled = lax.all_to_all(both, axis, split_axis=split_dim, concat_axis=concat_dim, tiled=True)
    return tuple(jnp.split(filled, [sum(widths[:k]) for k in range(1, len(widths))], axis=along))


def scatter_axes(shard, axes, dim):
    if not axes:
        return shard
    nearer = lax.psum_scatter(shard, axes[0], scatter_dimension=dim, tiled=True)
    return scatter_axes(nearer, axes[1:], dim)


def layer_norm(values, ln_gain, ln_bias):
    center = values - jnp.mean(values, axis=-1, keepdims=True)
    spread = jnp.mean(center * center, axis=-1, keepdims=True)
    return center * lax.rsqrt(spread + 1e-05) * ln_gain + ln_bias


def encode(inputs, qkv_full, out_full, ln_gain, ln_bias):
    passages = inputs.shape[0] // SEQ
    packed = jnp.dot(inputs, qkv_full, preferred_element_type=jnp.float32).astype(jnp.bfloat16)
    packed = packed.reshape(passages, SEQ, 3, HEADS, HEAD)
    scores = jnp.einsum(
        "bqhd,bkhd->bhqk", packed[:, :, 0], packed[:, :, 1], preferred_element_type=jnp.float32
    ) * (1.0 / math.sqrt(HEAD))
    probs = jax.nn.softmax(scores, axis=-1).astype(jnp.bfloat16)
    context = jnp.einsum(
        "bhqk,bkhd->bqhd", probs, packed[:, :, 2], preferred_element_type=jnp.float32
    )
    context = context.astype(jnp.bfloat16).reshape(inputs.shape[0], HEADS * HEAD)
    mixed = jnp.dot(context, out_full, preferred_element_type=jnp.float32) + inputs.astype(
        jnp.float32
    )
    return layer_norm(mixed, ln_gain, ln_bias).astype(jnp.bfloat16)


def shards(token_ids, embed_table, w_qkv, w_out, ln_gain, ln_bias, centroids_t, assignments):
    dp_size = lax.axis_size("dp")
    fsdp_size = lax.axis_size(FSDP)
    dp_rank = lax.axis_index("dp")
    fsdp_rank = lax.axis_index(FSDP)
    vocab_rows = embed_table.shape[0]
    local_ids = token_ids - fsdp_rank * vocab_rows
    inside = (local_ids >= 0) & (local_ids < vocab_rows)
    looked = jnp.take(embed_table, jnp.clip(local_ids, 0, vocab_rows - 1), axis=0)
    looked = jnp.where(inside[:, None], looked, jnp.zeros_like(looked))
    inputs = sent_and_summed(looked, FSDP, 0).astype(jnp.bfloat16)
    qkv_full, out_full, cent_full = in_one_piece((w_qkv, w_out, centroids_t), FSDP, 0, 1)
    encoded = encode(inputs, qkv_full, out_full, ln_gain, ln_bias)
    own_rows = encoded.shape[0]
    width = encoded.shape[1]
    block_width = cent_full.shape[1]
    per_dev = block_width // fsdp_size
    slab = lax.all_gather(encoded, "dp", axis=0, tiled=True)
    slab_assign = lax.dynamic_index_in_dim(
        assignments.reshape(dp_size, fsdp_size, own_rows), fsdp_rank, 1, keepdims=False
    ).reshape(-1)
    owned = slab_assign - dp_rank * block_width
    slab_rows = slab.shape[0]
    step_rows = math.gcd(slab_rows, 512)
    columns = jnp.arange(block_width, dtype=jnp.int32)

    def visit(totals, pieces):
        block_rows, local = pieces
        logits = jnp.dot(block_rows, cent_full, preferred_element_type=jnp.float32)
        peak = jnp.max(logits, axis=1)
        mass = jnp.sum(jnp.exp(logits - peak[:, None]), axis=1)
        hits = local[:, None] == columns[None, :]
        picked = jnp.sum(jnp.where(hits, logits, 0.0), axis=1)
        totals = totals + lax.dot_general(
            hits.astype(jnp.bfloat16),
            block_rows,
            (((0,), (0,)), ((), ())),
            preferred_element_type=jnp.float32,
        )
        return (totals, (peak, mass, picked))

    start = jnp.zeros((block_width, width), jnp.float32)
    partial_value, stats = lax.scan(
        visit,
        start,
        (
            slab.reshape(slab_rows // step_rows, step_rows, width),
            owned.reshape(slab_rows // step_rows, step_rows),
        ),
    )
    peaks, masses, picks = (stats[0].reshape(-1), stats[1].reshape(-1), stats[2].reshape(-1))
    got_peaks, got_masses, got_picks = sent_together(
        (
            peaks.reshape(dp_size, own_rows),
            masses.reshape(dp_size, own_rows),
            picks.reshape(dp_size, own_rows),
        ),
        "dp",
        0,
        0,
        1,
    )
    peak_own = jnp.max(got_peaks, axis=0)
    mass_own = jnp.sum(got_masses * jnp.exp(got_peaks - peak_own[None, :]), axis=0)
    pick_own = jnp.sum(got_picks, axis=0)
    token_loss = jnp.log(mass_own) + peak_own - pick_own
    totals = scatter_axes(partial_value, FSDP, 0)
    base = dp_rank * block_width + fsdp_rank * per_dev
    targets = base + jnp.arange(per_dev, dtype=jnp.int32)
    counts = jnp.sum((assignments[:, None] == targets[None, :]).astype(jnp.int32), axis=0)
    previous = lax.dynamic_slice_in_dim(cent_full, fsdp_rank * per_dev, per_dev, 1).T.astype(
        jnp.float32
    )
    new_centroids = jnp.where(
        counts[:, None] > 0, totals / jnp.maximum(counts, 1)[:, None].astype(jnp.float32), previous
    )
    return (token_loss, new_centroids)


def solution(mesh):
    finer = Mesh(mesh.devices.reshape(mesh.shape["dp"], 4, 4), ("dp", "fsdp_0", "fsdp_1"))
    placed = (P("dp"), P(FSDP, None), P(FSDP, None), P(FSDP, None), P(), P(), P(FSDP, "dp"), P())
    return jax.shard_map(
        shards,
        mesh=finer,
        in_specs=placed,
        out_specs=(P(DP_FSDP), P(DP_FSDP, None)),
        check_vma=False,
    )
```

profile of v0, /device:TPU:1, one launch (start us, length us, event | category | flops | bytes accessed | tf_op | source)
XLA Modules:
  0.0 507.1 jit_solution(12758839840471704334)
XLA Ops:
  7.2 2.1 pad_maximum_fusion
  10.1 9.5 %gather_fusion = bf16[2048,768]{1,0:T(8,128)(2,1)} fusion(bf16[1908,768]{1,0:T(8,128)(2,1)S(1)} %copy-done, s32[2048]{0:T(1024)S(1)} %fusion.19), kind=kCustom, calls=%fused_computation | custom fusion | bytes 6299648 | tf_op jit(solution)/shard_map/jit(_take)/gather | solution.py:81
  19.6 2.3 select_select_fusion
  21.8 157.9 %all_to_all.17 = bf16[16,128,768]{2,1,0:T(8,128)(2,1)} all-to-all(bf16[16,128,768]{2,1,0:T(8,128)(2,1)S(1)} %select_select_fusion), channel_id=1, replica_groups=mesh['dp'=16,'fsdp_0'=4,'fsdp_1'=4] {'fsdp_0','fsdp_1'}, dimensions={0} | all-to-all | bytes 6291456 | tf_op jit(solution)/shard_map/all_to_all | solution.py:22
  179.7 2.3 reduce_sum.84
  182.1 69.7 %all-gather.3.cloned.1.call-done = bf16[768,5120]{1,0:T(8,128)(2,1)} async-done(((bf16[48,5120]{1,0:T(8,128)(2,1)}), bf16[768,5120]{1,0:T(8,128)(2,1)}) %all-gather.3.cloned.1.call-update) | async-done | bytes 7864336 | tf_op jit(solution)/shard_map/all_gather | solution.py:28
  251.8 3.5 convolution_convert_fusion
  255.3 1.4 copy.28
  256.7 1.3 convolution_multiply_fusion
  258.4 2.5 convolution_convert_fusion.1
  260.9 1.8 fusion.24
  264.8 3.9 slice.31
  268.7 66.8 %all-gather.5.cloned.1.call-done = bf16[2048,768]{1,0:T(8,128)(2,1)} async-done(((bf16[128,768]{1,0:T(8,128)(2,1)}), bf16[2048,768]{1,0:T(8,128)(2,1)}) %all-gather.5.cloned.1.call-update) | async-done | bytes 3145744 | tf_op jit(solution)/shard_map/all_gather | solution.py:90
  335.5 51.3 %while.17 = (s32[]{:T(128)}, f32[2048,768]{1,0:T(8,128)}, f32[4,512]{1,0:T(4,128)S(1)}, f32[4,512]{1,0:T(4,128)S(1)}, f32[4,512]{1,0:T(4,128)S(1)}, /*index=5*/s...) while((s32[]{:T(128)}, f32[2048,768]{1,0:T(8,128)}, ...), condition=%wide.region_9.10_spmd.clone, body=%wide.region_5.9_spmd.clone.sunk | while | flops 3231709696 | bytes 25719936 | solution.py:115
  335.5 4.0 fusion.35
  339.5 1.4 fusion.36
  341.0 5.8 %select_add_fusion.2 = f32[2048,768]{1,0:T(8,128)} fusion(f32[2048,768]{1,0:T(8,128)} %get-tuple-element.199, pred[]{:T(512)S(6)} %compare.3, s32[512]{0:T(512)S(1)} %bitcast.70, bf16[4,512,768]{2,1,0:T(8,128)(2,1)} %get-tuple-element.214, s32[]{:T(128)} %get-tuple-element.198), kind=kOutput, calls=%fused_computation.2.clone.1 | convolution fusion | flops 1614807040 | bytes 13371905 | tf_op jit(solution)/shard_map/while/body/eval_jaxpr/dot_general | solution.py:106
  346.9 4.0 fusion.35
  350.9 1.4 fusion.36
  352.4 7.7 %select_add_fusion.2 = f32[2048,768]{1,0:T(8,128)} fusion(f32[2048,768]{1,0:T(8,128)} %get-tuple-element.199, pred[]{:T(512)S(6)} %compare.3, s32[512]{0:T(512)S(1)} %bitcast.70, bf16[4,512,768]{2,1,0:T(8,128)(2,1)} %get-tuple-element.214, s32[]{:T(128)} %get-tuple-element.198), kind=kOutput, calls=%fused_computation.2.clone.1 | convolution fusion | flops 1614807040 | bytes 13371905 | tf_op jit(solution)/shard_map/while/body/eval_jaxpr/dot_general | solution.py:106
  360.2 4.0 fusion.35
  364.2 1.4 fusion.36
  365.7 7.7 %select_add_fusion.2 = f32[2048,768]{1,0:T(8,128)} fusion(f32[2048,768]{1,0:T(8,128)} %get-tuple-element.199, pred[]{:T(512)S(6)} %compare.3, s32[512]{0:T(512)S(1)} %bitcast.70, bf16[4,512,768]{2,1,0:T(8,128)(2,1)} %get-tuple-element.214, s32[]{:T(128)} %get-tuple-element.198), kind=kOutput, calls=%fused_computation.2.clone.1 | convolution fusion | flops 1614807040 | bytes 13371905 | tf_op jit(solution)/shard_map/while/body/eval_jaxpr/dot_general | solution.py:106
  373.5 4.0 fusion.35
  377.5 1.4 fusion.36
  379.0 7.7 %select_add_fusion.2 = f32[2048,768]{1,0:T(8,128)} fusion(f32[2048,768]{1,0:T(8,128)} %get-tuple-element.199, pred[]{:T(512)S(6)} %compare.3, s32[512]{0:T(512)S(1)} %bitcast.70, bf16[4,512,768]{2,1,0:T(8,128)(2,1)} %get-tuple-element.214, s32[]{:T(128)} %get-tuple-element.198), kind=kOutput, calls=%fused_computation.2.clone.1 | convolution fusion | flops 1614807040 | bytes 13371905 | tf_op jit(solution)/shard_map/while/body/eval_jaxpr/dot_general | solution.py:106
  386.8 6.6 %copy.30 = f32[2048,768]{0,1:T(8,128)} copy(f32[2048,768]{1,0:T(8,128)} %get-tuple-element.55) | data formatting | bytes 12582912 | tf_op jit(solution)/shard_map/while | solution.py:115
  393.5 62.0 %reduce-scatter.3.cloned.1.call-done = f32[512,768]{0,1:T(8,128)} async-done(((f32[2048,768]{0,1:T(8,128)}), f32[512,768]{0,1:T(8,128)}) %reduce-scatter.3.cloned.1.call-update) | async-done | bytes 1572880 | tf_op jit(solution)/shard_map/reduce_scatter | solution.py:45
  455.5 5.6 %convert_reduce_fusion = s32[128]{0:T(128)S(1)} fusion(s32[128]{0:T(128)S(1)} %iota_add_fusion, s32[32768]{0:T(1024)S(1)} %copy-done.2), kind=kLoop, calls=%fused_computation.18 | loop fusion | flops 12582784 | bytes 132096 | tf_op jit(solution)/shard_map/reduce_sum | solution.py:142
  461.8 10.1 %all-to-all-start.1 = ((f32[16,1,384]{2,1,0:T(1,128)}), f32[16,1,384]{2,1,0:T(1,128)S(1)}, u32[]{:S(2)}, u32[]{:S(2)}) async-start(f32[16,1,384]{2,1,0:T(1,128)} %all_to_all.12), calls=%async_computation.1 | async-start | bytes 49152 | tf_op jit(solution)/shard_map/all_to_all | solution.py:38
  471.9 9.7 %all-to-all-done.1 = f32[16,1,384]{2,1,0:T(1,128)S(1)} async-done(((f32[16,1,384]{2,1,0:T(1,128)}), f32[16,1,384]{2,1,0:T(1,128)S(1)}, u32[]{:S(2)}, u32[]{:S(2)}) %all-to-all-start.1) | async-done | bytes 24608 | tf_op jit(solution)/shard_map/all_to_all | solution.py:38
  482.2 16.4 %reduce-scatter.5.cloned.1.call-done = f32[128,768]{0,1:T(8,128)} async-done(((f32[512,768]{0,1:T(8,128)}), f32[128,768]{0,1:T(8,128)}) %reduce-scatter.5.cloned.1.call-update) | async-done | bytes 393232 | tf_op jit(solution)/shard_map/reduce_scatter | solution.py:45
  (63 shorter events, 7.2 us)
Async XLA Ops:
  7.2 2.9 copy-start
  7.2 244.6 %all-gather.3.cloned.1.call-start = ((), (), s32[]{:S(2)}) async-start(), calls=%async_computation.4 | async-start | bytes 8355840 | tf_op jit(solution)/shard_map/all_gather | solution.py:28
  9.3 326.2 %all-gather.5.cloned.1.call-start = ((), (), s32[]{:S(2)}) async-start(), calls=%async_computation.5 | async-start | bytes 3342336 | tf_op jit(solution)/shard_map/all_gather | solution.py:90
  10.1 9.5 %copy-start.3 = (s32[2048]{0:T(1024)S(1)}, s32[2048]{0:T(1024)}, u32[]{:S(2)}) copy-start(s32[2048]{0:T(1024)} %param.10) | copy-start | bytes 24580
  182.1 69.7 %copy-start.1 = (bf16[128,768]{1,0:T(8,128)(2,1)}, bf16[128,768]{1,0:T(8,128)(2,1)S(1)}, u32[]{:S(2)}) copy-start(bf16[128,768]{1,0:T(8,128)(2,1)S(1)} %reduce_sum.84) | copy-start | bytes 589828
  256.7 6.3 %copy-start.4 = (f32[768]{0:T(1024)S(1)}, f32[768]{0:T(1024)}, u32[]{:S(2)}) copy-start(f32[768]{0:T(1024)} %param.15) | copy-start | bytes 9220
  256.7 6.3 %copy-start.5 = (f32[768]{0:T(1024)S(1)}, f32[768]{0:T(1024)}, u32[]{:S(2)}) copy-start(f32[768]{0:T(1024)} %param.14) | copy-start | bytes 9220
  263.8 191.7 %reduce-scatter.3.cloned.1.call-start = ((), (), s32[]{:S(2)}) async-start(), calls=%async_computation.6 | async-start | bytes 7864320 | tf_op jit(solution)/shard_map/reduce_scatter | solution.py:45
  393.4 62.1 %copy-start.2 = (s32[32768]{0:T(1024)S(1)}, s32[32768]{0:T(1024)}, u32[]{:S(2)}) copy-start(s32[32768]{0:T(1024)} %param.17) | copy-start | bytes 393220
  393.4 105.2 %reduce-scatter.5.cloned.1.call-start = ((), (), s32[]{:S(2)}) async-start(), calls=%async_computation.7 | async-start | bytes 1966080 | tf_op jit(solution)/shard_map/reduce_scatter | solution.py:45
  461.8 19.8 %all-to-all-start.1 = ((f32[16,1,384]{2,1,0:T(1,128)}), f32[16,1,384]{2,1,0:T(1,128)S(1)}, u32[]{:S(2)}, u32[]{:S(2)}) async-start(f32[16,1,384]{2,1,0:T(1,128)} %all_to_all.12), calls=%async_computation.1 | async-start | bytes 49152 | tf_op jit(solution)/shard_map/all_to_all | solution.py:38
Sparse Core Ops, SparseCore 0:
  9.8 241.9 all-gather.2
  263.9 71.5 all-gather.4
  393.5 61.9 reduce-scatter.2
  457.9 40.6 reduce-scatter.4
where the time goes:
time: 508 us; the launch traced here: 507 us
  waiting for transfers between devices  225 us (44%)
  blocking collectives  158 us (31%)
  matrix products  54.5 us (11%)
  local copies, waits for them, and re-layouts  23.6 us (5%)
  other arithmetic  22.2 us (4%)
  between operations  14 us (3%)
  starting transfers between devices  10.2 us (2%)
    all_to_all x1, blocking collectives, sent_and_summed(): lax.all_to_all(in_blocks(shard, dim, devices), axis, 0, 0, tiled=True)  158 us
    reduce_scatter x2, waiting for transfers between devices, scatter_axes(): nearer = lax.psum_scatter(shard, axes[0], scatter_dimension=dim, tiled=True)  78.4 us
    all_gather x1, waiting for transfers between devices, in_one_piece(): filled, at, done = (lax.all_gather(both, axis, axis=dim, tiled=True), 0, [])  69.7 us
    all_gather x1, waiting for transfers between devices, shards(): slab = lax.all_gather(encoded, 'dp', axis=0, tiled=True)  66.8 us
    dot_general x4, matrix products, visit(): lax.dot_general(hits.astype(jnp.bfloat16), block_rows, (((0,), (0,)), (()...  28.8 us
    dot_general x4, matrix products, visit(): logits = jnp.dot(block_rows, cent_full, preferred_element_type=jnp.float32)  16.1 us
  transfers between devices with their start and end apart: 5, of which 5 were waited for; matrix products, arithmetic and copies ran while one was open for 5% of the time, Pallas kernels for 0%

commit v1 on v0

--- a/solution.py
+++ b/solution.py
@@ -87,7 +87,9 @@
     width = encoded.shape[1]
     block_width = cent_full.shape[1]
     per_dev = block_width // fsdp_size
-    slab = lax.all_gather(encoded, "dp", axis=0, tiled=True)
+    slab = jnp.concatenate(
+        lax.all_to_all(jnp.stack([encoded] * lax.axis_size("dp")), "dp", 0, 0), axis=0
+    )
     slab_assign = lax.dynamic_index_in_dim(
         assignments.reshape(dp_size, fsdp_size, own_rows), fsdp_rank, 1, keepdims=False
     ).reshape(-1)

time: 508 us -> 531 us (1.045)
  waiting for transfers between devices: 225 us -> 238 us
  starting transfers between devices: 10.2 us -> 20 us
    all_gather x1 -> x0, waiting for transfers between devices: 66.8 us -> none  [shards(): slab = lax.all_gather(encoded, 'dp', axis=0, tiled=True)]
    reduce_scatter x2, waiting for transfers between devices: 78.4 us -> 121 us  [scatter_axes(): nearer = lax.psum_scatter(shard, axes[0], scatter_dimension=dim, tiled=True)]
    all_to_all x0 -> x1, waiting for transfers between devices: none -> 38.3 us  [shards(): lax.all_to_all(jnp.stack([encoded] * lax.axis_size('dp')), 'dp', 0, 0)]
    all_to_all x0 -> x1, starting transfers between devices: none -> 9.83 us  [shards(): lax.all_to_all(jnp.stack([encoded] * lax.axis_size('dp')), 'dp', 0, 0)]
where the time goes in v1:
time: 531 us; the launch traced here: 530 us
  waiting for transfers between devices  238 us (45%)
  blocking collectives  158 us (30%)
  matrix products  54.5 us (10%)
  local copies, waits for them, and re-layouts  25.6 us (5%)
  other arithmetic  20.7 us (4%)
  starting transfers between devices  20 us (4%)
  between operations  14 us (3%)
    all_to_all x1, blocking collectives, sent_and_summed(): lax.all_to_all(in_blocks(shard, dim, devices), axis, 0, 0, tiled=True)  158 us
    reduce_scatter x2, waiting for transfers between devices, scatter_axes(): nearer = lax.psum_scatter(shard, axes[0], scatter_dimension=dim, tiled=True)  121 us
    all_gather x1, waiting for transfers between devices, in_one_piece(): filled, at, done = (lax.all_gather(both, axis, axis=dim, tiled=True), 0, [])  69.1 us
    all_to_all x1, waiting for transfers between devices, shards(): lax.all_to_all(jnp.stack([encoded] * lax.axis_size('dp')), 'dp', 0, 0)  38.3 us
    dot_general x4, matrix products, visit(): lax.dot_general(hits.astype(jnp.bfloat16), block_rows, (((0,), (0,)), (()...  28.8 us
    dot_general x4, matrix products, visit(): logits = jnp.dot(block_rows, cent_full, preferred_element_type=jnp.float32)  16.1 us
  transfers between devices with their start and end apart: 5, of which 5 were waited for; matrix products, arithmetic and copies ran while one was open for 5% of the time, Pallas kernels for 0%

profile of v1, /device:TPU:1, one launch (start us, length us, event | category | flops | bytes accessed | tf_op | source)
XLA Modules:
  0.0 530.4 jit_solution(1938286921218316801)
XLA Ops:
  7.2 2.1 pad_maximum_fusion
  10.0 9.5 %gather_fusion = bf16[2048,768]{1,0:T(8,128)(2,1)} fusion(bf16[1908,768]{1,0:T(8,128)(2,1)S(1)} %copy-done, s32[2048]{0:T(1024)S(1)} %fusion.19), kind=kCustom, calls=%fused_computation | custom fusion | bytes 6299648 | tf_op jit(solution)/shard_map/jit(_take)/gather | solution.py:81
  19.5 2.3 select_select_fusion
  21.8 157.9 %all_to_all.22 = bf16[16,128,768]{2,1,0:T(8,128)(2,1)} all-to-all(bf16[16,128,768]{2,1,0:T(8,128)(2,1)S(1)} %select_select_fusion), channel_id=1, replica_groups=mesh['dp'=16,'fsdp_0'=4,'fsdp_1'=4] {'fsdp_0','fsdp_1'}, dimensions={0} | all-to-all | bytes 6291456 | tf_op jit(solution)/shard_map/all_to_all | solution.py:22
  179.7 2.3 reduce_sum.84
  182.0 69.1 %all-gather.2.cloned.1.call-done = bf16[768,5120]{1,0:T(8,128)(2,1)} async-done(((bf16[48,5120]{1,0:T(8,128)(2,1)}), bf16[768,5120]{1,0:T(8,128)(2,1)}) %all-gather.2.cloned.1.call-update) | async-done | bytes 7864336 | tf_op jit(solution)/shard_map/all_gather | solution.py:28
  251.1 3.5 convolution_convert_fusion
  257.7 2.5 convolution_convert_fusion.1
  260.3 1.8 fusion.24
  262.4 2.0 stack.2
  264.4 9.8 %all-to-all-start.1 = ((bf16[16,128,768]{2,1,0:T(8,128)(2,1)}), bf16[16,128,768]{2,1,0:T(8,128)(2,1)}, u32[]{:S(2)}, u32[]{:S(2)}) async-start(bf16[16,128,768]{2,1,0:T(8,128)(2,1)} %stack.2), calls=%async_computation.1 | async-start | bytes 6291456 | tf_op jit(solution)/shard_map/all_to_all | solution.py:91
  274.4 3.9 slice.31
  278.3 38.3 %all-to-all-done.1 = bf16[16,128,768]{2,1,0:T(8,128)(2,1)} async-done(((bf16[16,128,768]{2,1,0:T(8,128)(2,1)}), bf16[16,128,768]{2,1,0:T(8,128)(2,1)}, u32[]{:S(2)}, u32[]{:S(2)}) %all-to-all-start.1) | async-done | bytes 3145760 | tf_op jit(solution)/shard_map/all_to_all | solution.py:91
  316.7 51.3 %while.17 = (s32[]{:T(128)}, f32[2048,768]{1,0:T(8,128)}, f32[4,512]{1,0:T(4,128)S(1)}, f32[4,512]{1,0:T(4,128)S(1)}, f32[4,512]{1,0:T(4,128)S(1)}, /*index=5*/s...) while((s32[]{:T(128)}, f32[2048,768]{1,0:T(8,128)}, ...), condition=%wide.region_9.10_spmd.clone, body=%wide.region_5.9_spmd.clone.sunk | while | flops 3231709696 | bytes 25719936 | solution.py:117
  316.7 4.0 fusion.35
  320.7 1.4 fusion.36
  322.2 5.8 %select_add_fusion.2 = f32[2048,768]{1,0:T(8,128)} fusion(f32[2048,768]{1,0:T(8,128)} %get-tuple-element.199, pred[]{:T(512)S(6)} %compare.3, s32[512]{0:T(512)S(1)} %bitcast.69, bf16[4,512,768]{2,1,0:T(8,128)(2,1)} %get-tuple-element.214, s32[]{:T(128)} %get-tuple-element.198), kind=kOutput, calls=%fused_computation.2.clone.1 | convolution fusion | flops 1614807040 | bytes 13371905 | tf_op jit(solution)/shard_map/while/body/eval_jaxpr/dot_general | solution.py:108
  328.1 4.0 fusion.35
  332.1 1.4 fusion.36
  333.6 7.7 %select_add_fusion.2 = f32[2048,768]{1,0:T(8,128)} fusion(f32[2048,768]{1,0:T(8,128)} %get-tuple-element.199, pred[]{:T(512)S(6)} %compare.3, s32[512]{0:T(512)S(1)} %bitcast.69, bf16[4,512,768]{2,1,0:T(8,128)(2,1)} %get-tuple-element.214, s32[]{:T(128)} %get-tuple-element.198), kind=kOutput, calls=%fused_computation.2.clone.1 | convolution fusion | flops 1614807040 | bytes 13371905 | tf_op jit(solution)/shard_map/while/body/eval_jaxpr/dot_general | solution.py:108
  341.3 4.0 fusion.35
  345.4 1.4 fusion.36
  346.9 7.7 %select_add_fusion.2 = f32[2048,768]{1,0:T(8,128)} fusion(f32[2048,768]{1,0:T(8,128)} %get-tuple-element.199, pred[]{:T(512)S(6)} %compare.3, s32[512]{0:T(512)S(1)} %bitcast.69, bf16[4,512,768]{2,1,0:T(8,128)(2,1)} %get-tuple-element.214, s32[]{:T(128)} %get-tuple-element.198), kind=kOutput, calls=%fused_computation.2.clone.1 | convolution fusion | flops 1614807040 | bytes 13371905 | tf_op jit(solution)/shard_map/while/body/eval_jaxpr/dot_general | solution.py:108
  354.7 4.0 fusion.35
  358.7 1.4 fusion.36
  360.2 7.7 %select_add_fusion.2 = f32[2048,768]{1,0:T(8,128)} fusion(f32[2048,768]{1,0:T(8,128)} %get-tuple-element.199, pred[]{:T(512)S(6)} %compare.3, s32[512]{0:T(512)S(1)} %bitcast.69, bf16[4,512,768]{2,1,0:T(8,128)(2,1)} %get-tuple-element.214, s32[]{:T(128)} %get-tuple-element.198), kind=kOutput, calls=%fused_computation.2.clone.1 | convolution fusion | flops 1614807040 | bytes 13371905 | tf_op jit(solution)/shard_map/while/body/eval_jaxpr/dot_general | solution.py:108
  367.9 6.6 %copy.30 = f32[2048,768]{0,1:T(8,128)} copy(f32[2048,768]{1,0:T(8,128)} %get-tuple-element.55) | data formatting | bytes 12582912 | tf_op jit(solution)/shard_map/while | solution.py:117
  374.6 104.0 %reduce-scatter.3.cloned.1.call-done = f32[512,768]{0,1:T(8,128)} async-done(((f32[2048,768]{0,1:T(8,128)}), f32[512,768]{0,1:T(8,128)}) %reduce-scatter.3.cloned.1.call-update) | async-done | bytes 1572880 | tf_op jit(solution)/shard_map/reduce_scatter | solution.py:45
  478.6 5.6 %convert_reduce_fusion = s32[128]{0:T(128)S(1)} fusion(s32[128]{0:T(128)S(1)} %iota_add_fusion, s32[32768]{0:T(1024)S(1)} %copy-done.2), kind=kLoop, calls=%fused_computation.18 | loop fusion | flops 12582784 | bytes 132096 | tf_op jit(solution)/shard_map/reduce_sum | solution.py:144
  485.0 10.1 %all-to-all-start.2 = ((f32[16,1,384]{2,1,0:T(1,128)}), f32[16,1,384]{2,1,0:T(1,128)S(1)}, u32[]{:S(2)}, u32[]{:S(2)}) async-start(f32[16,1,384]{2,1,0:T(1,128)} %all_to_all.16), calls=%async_computation.2 | async-start | bytes 49152 | tf_op jit(solution)/shard_map/all_to_all | solution.py:38
  495.0 9.7 %all-to-all-done.2 = f32[16,1,384]{2,1,0:T(1,128)S(1)} async-done(((f32[16,1,384]{2,1,0:T(1,128)}), f32[16,1,384]{2,1,0:T(1,128)S(1)}, u32[]{:S(2)}, u32[]{:S(2)}) %all-to-all-start.2) | async-done | bytes 24608 | tf_op jit(solution)/shard_map/all_to_all | solution.py:38
  505.3 16.6 %reduce-scatter.5.cloned.1.call-done = f32[128,768]{0,1:T(8,128)} async-done(((f32[512,768]{0,1:T(8,128)}), f32[128,768]{0,1:T(8,128)}) %reduce-scatter.5.cloned.1.call-update) | async-done | bytes 393232 | tf_op jit(solution)/shard_map/reduce_scatter | solution.py:45
  (63 shorter events, 8.2 us)
Async XLA Ops:
  7.2 2.9 copy-start
  7.2 243.9 %all-gather.2.cloned.1.call-start = ((), (), s32[]{:S(2)}) async-start(), calls=%async_computation.5 | async-start | bytes 8355840 | tf_op jit(solution)/shard_map/all_gather | solution.py:28
  10.0 9.5 %copy-start.3 = (s32[2048]{0:T(1024)S(1)}, s32[2048]{0:T(1024)}, u32[]{:S(2)}) copy-start(s32[2048]{0:T(1024)} %param.10) | copy-start | bytes 24580
  182.0 69.1 %copy-start.1 = (bf16[128,768]{1,0:T(8,128)(2,1)}, bf16[128,768]{1,0:T(8,128)(2,1)S(1)}, u32[]{:S(2)}) copy-start(bf16[128,768]{1,0:T(8,128)(2,1)S(1)} %reduce_sum.84) | copy-start | bytes 589828
  257.3 5.0 copy-start.4
  257.3 5.0 copy-start.5
  264.4 9.9 %copy-start.2 = (s32[32768]{0:T(1024)S(1)}, s32[32768]{0:T(1024)}, u32[]{:S(2)}) copy-start(s32[32768]{0:T(1024)} %param.17) | copy-start | bytes 393220
  264.4 52.3 %all-to-all-start.1 = ((bf16[16,128,768]{2,1,0:T(8,128)(2,1)}), bf16[16,128,768]{2,1,0:T(8,128)(2,1)}, u32[]{:S(2)}, u32[]{:S(2)}) async-start(bf16[16,128,768]{2,1,0:T(8,128)(2,1)} %stack.2), calls=%async_computation.1 | async-start | bytes 6291456 | tf_op jit(solution)/shard_map/all_to_all | solution.py:91
  274.3 204.3 %reduce-scatter.3.cloned.1.call-start = ((), (), s32[]{:S(2)}) async-start(), calls=%async_computation.6 | async-start | bytes 7864320 | tf_op jit(solution)/shard_map/reduce_scatter | solution.py:45
  374.6 147.3 %reduce-scatter.5.cloned.1.call-start = ((), (), s32[]{:S(2)}) async-start(), calls=%async_computation.7 | async-start | bytes 1966080 | tf_op jit(solution)/shard_map/reduce_scatter | solution.py:45
  485.0 19.8 %all-to-all-start.2 = ((f32[16,1,384]{2,1,0:T(1,128)}), f32[16,1,384]{2,1,0:T(1,128)S(1)}, u32[]{:S(2)}, u32[]{:S(2)}) async-start(f32[16,1,384]{2,1,0:T(1,128)} %all_to_all.16), calls=%async_computation.2 | async-start | bytes 49152 | tf_op jit(solution)/shard_map/all_to_all | solution.py:38
Sparse Core Ops, SparseCore 0:
  9.8 241.2 all-gather.1
  374.7 103.8 reduce-scatter.2
  481.2 40.6 reduce-scatter.4
